TPU v7x, 512 devices: a whole 4x4x16 slice. The times are simulated.
512 devices in a mesh: rep: 4 (over x), tm: 16 (over z), height: 8 (over y, core).
Axes of the slice: x: 4, y: 4, z: 16, core: 2. Of those that a mesh axis runs over, the one named last changes fastest.
Arguments:
- inputs: bfloat16 [4, 64, 128, 32, 128], P('rep', 'tm', 'height'), may hold values from -32 to 32
- spatial_kernel: bfloat16 [3, 3, 128, 128], replicated, may hold values from -0.1875 to 0.1875
- temporal_kernel: bfloat16 [3, 128, 128], replicated, may hold values from -0.3125 to 0.3125
- norm_gain: float32 [128], replicated, may hold values from 0.1 to 1.9
- norm_shift: float32 [128], replicated, may hold values from -3 to 3
- cotangent: bfloat16 [4, 64, 128, 32, 128], P('rep', 'tm', 'height'), may hold values from -6 to 6
Outputs:
- outputs: bfloat16 [4, 64, 128, 32, 128], P('rep', 'tm', 'height')
- grad_inputs: bfloat16 [4, 64, 128, 32, 128], P('rep', 'tm', 'height')
- grad_spatial: float32 [3, 3, 128, 128], replicated
- grad_temporal: float32 [3, 128, 128], replicated
- grad_gain: float32 [128], replicated
- grad_shift: float32 [128], replicated
All inputs are finite; a program needn't handle non-finite values.
Results may differ from a plain program's by a relative error of at most 0.0041.
The roundings to bfloat16 on the way count: a program that leaves them out, or rounds other values in their place, can miss the bound.
Values may be sent and summed in bfloat16 or wider, within the bound.
No kernel may reach another device: no remote copies, remote signals or barrier semaphores. Data moves between devices by JAX's collectives and lax.ppermute only.
A program may use at most 64 MiB of HBM per device.

v0:
```python
import math
import jax
import jax.numpy as jnp
from jax import lax
from jax.sharding import PartitionSpec as P

GROUPS = 32
EPS = 1e-05


def with_halo(value, sides, width):
    for axis, dim in sides:
        count, length = (lax.axis_size(axis), value.shape[dim])
        up = [(i, (i + 1) % count) for i in range(count - 1)]
        down = [(j, i) for i, j in up]
        last = lax.slice_in_dim(value, length - width, length, axis=dim)
        first = lax.slice_in_dim(value, 0, width, axis=dim)
        before = lax.ppermute(last, axis, up)
        after = lax.ppermute(first, axis, down)
        value = jnp.concatenate([before, value, after], axis=dim)
    return value


def from_behind(value, axis, steps):
    count = lax.axis_size(axis)
    first, last = (max(0, -steps), min(count, count - steps))
    return lax.ppermute(value, axis, [(source, source + steps) for source in range(first, last)])


def carried_in(part, axis, combine, identity, reverse):
    count = lax.axis_size(axis)
    place = lax.axis_index(axis)
    ahead = count - 1 - place if reverse else place
    gathered = jax.tree.map(lambda a: lax.all_gather(a, axis), part)
    state = jax.tree.map(lambda a, e: jnp.zeros_like(a) + jnp.asarray(e, a.dtype), part, identity)

    def one(turn, state):
        source = count - 1 - turn if reverse else turn
        return combine(
            state, jax.tree.map(lambda a: lax.dynamic_index_in_dim(a, source, 0, False), gathered)
        )

    return lax.fori_loop(0, ahead, one, state)


def add_pair(earlier, later):
    return (earlier[0] + later[0], earlier[1] + later[1])


def reverse_sum(values):
    return jnp.cumsum(values[::-1], 0)[::-1]


def widen(stat):
    return stat[:, None, None, :, None]


def shards(inputs, spatial_kernel, temporal_kernel, norm_gain, norm_shift, cotangent):
    pixels_in = inputs[0]
    frames, rows, columns, channels = pixels_in.shape
    group_size = channels // GROUPS
    time_devices = lax.axis_size("tm")
    height_devices = lax.axis_size("height")
    frame_start = lax.axis_index("tm") * frames
    per_frame = float(rows * height_devices * columns * group_size)
    halo_in = with_halo(pixels_in, (("height", 1),), 1)
    padded = jnp.pad(halo_in, ((0, 0), (0, 0), (1, 1), (0, 0)))
    total = jnp.zeros((frames, rows, columns, channels), jnp.float32)
    for row_tap in range(3):
        for col_tap in range(3):
            window = padded[:, row_tap : row_tap + rows, col_tap : col_tap + columns]
            total = total + jnp.einsum(
                "frwc,cd->frwd",
                window,
                spatial_kernel[row_tap, col_tap],
                preferred_element_type=jnp.float32,
            )
    feature = total.astype(jnp.bfloat16)
    prior = from_behind(feature[frames - 2 :], "tm", 1)
    earlier = jnp.concatenate([prior, feature], 0)
    mixed = jnp.zeros((frames, rows, columns, channels), jnp.float32)
    for time_tap in range(3):
        mixed = mixed + jnp.einsum(
            "frwc,cd->frwd",
            earlier[time_tap : time_tap + frames],
            temporal_kernel[time_tap],
            preferred_element_type=jnp.float32,
        )
    grouped = mixed.reshape(frames, rows, columns, GROUPS, group_size)
    first = grouped.sum((1, 2, 4))
    second = (grouped * grouped).sum((1, 2, 4))
    row_first, row_second = lax.psum((first, second), "height")
    empty = jnp.zeros((GROUPS,), jnp.float32)
    before = carried_in(
        (row_first.sum(0), row_second.sum(0)), "tm", add_pair, (empty, empty), False
    )
    counted = ((frame_start + jnp.arange(frames)).astype(jnp.float32) + 1.0)[:, None] * per_frame
    mean = (before[0] + jnp.cumsum(row_first, 0)) / counted
    variance = (before[1] + jnp.cumsum(row_second, 0)) / counted - mean * mean
    inv_std = lax.rsqrt(variance + EPS)
    normed = (grouped - widen(mean)) * widen(inv_std)
    gain = norm_gain.reshape(GROUPS, group_size)
    shift = norm_shift.reshape(GROUPS, group_size)
    pre = normed * gain + shift
    sigma = jax.nn.sigmoid(pre)
    outputs = (
        pixels_in.astype(jnp.float32) + (pre * sigma).reshape(frames, rows, columns, channels)
    ).astype(jnp.bfloat16)
    grad_pre = cotangent[0].astype(jnp.float32).reshape(grouped.shape) * (
        sigma * (1.0 + pre * (1.0 - sigma))
    )
    gain_part = (grad_pre * normed).sum((0, 1, 2)).reshape(channels)
    shift_part = grad_pre.sum((0, 1, 2)).reshape(channels)
    grad_normed = grad_pre * gain
    local_a = grad_normed.sum((1, 2, 4))
    local_b = (grad_normed * normed).sum((1, 2, 4))
    sum_a, sum_b = lax.psum((local_a, local_b), "height")
    q_first = (-inv_std * sum_a + inv_std * inv_std * sum_b * mean) / counted
    q_second = -inv_std * inv_std * sum_b / (2.0 * counted)
    zeroed = jnp.zeros((GROUPS,), jnp.float32)
    after = carried_in((q_first.sum(0), q_second.sum(0)), "tm", add_pair, (zeroed, zeroed), True)
    carry_first = after[0] + reverse_sum(q_first)
    carry_second = after[1] + reverse_sum(q_second)
    grad_mixed = (
        widen(inv_std) * grad_normed + widen(carry_first) + 2.0 * grouped * widen(carry_second)
    )
    grad_mixed = grad_mixed.reshape(frames, rows, columns, channels).astype(jnp.bfloat16)
    temporal_terms = []
    for time_tap in range(3):
        temporal_terms.append(
            jnp.einsum(
                "frwc,frwd->cd",
                earlier[time_tap : time_tap + frames],
                grad_mixed,
                preferred_element_type=jnp.float32,
            )
        )
    temporal_part = jnp.stack(temporal_terms)
    following = from_behind(grad_mixed[:2], "tm", -1)
    later = jnp.concatenate([grad_mixed, following], 0)
    grad_feature = jnp.zeros((frames, rows, columns, channels), jnp.float32)
    for time_tap in range(3):
        grad_feature = grad_feature + jnp.einsum(
            "frwd,cd->frwc",
            later[2 - time_tap : 2 - time_tap + frames],
            temporal_kernel[time_tap],
            preferred_element_type=jnp.float32,
        )
    grad_feature = grad_feature.astype(jnp.bfloat16)
    halo_grad = with_halo(grad_feature, (("height", 1),), 1)
    padded_grad = jnp.pad(halo_grad, ((0, 0), (0, 0), (1, 1), (0, 0)))
    grad_in = cotangent[0].astype(jnp.float32)
    spatial_terms = []
    for row_tap in range(3):
        for col_tap in range(3):
            back = padded_grad[
                :, 2 - row_tap : 2 - row_tap + rows, 2 - col_tap : 2 - col_tap + columns
            ]
            grad_in = grad_in + jnp.einsum(
                "frwd,cd->frwc",
                back,
                spatial_kernel[row_tap, col_tap],
                preferred_element_type=jnp.float32,
            )
            window = padded[:, row_tap : row_tap + rows, col_tap : col_tap + columns]
            spatial_terms.append(
                jnp.einsum(
                    "frwc,frwd->cd", window, grad_feature, preferred_element_type=jnp.float32
                )
            )
    spatial_part = jnp.stack(spatial_terms).reshape(3, 3, channels, channels)
    grad_inputs = grad_in.astype(jnp.bfloat16)
    spatial_sum, temporal_sum, gain_sum, shift_sum = lax.psum(
        (spatial_part, temporal_part, gain_part, shift_part), ("rep", "tm", "height")
    )
    pixel_total = lax.axis_size("rep") * frames * time_devices * rows * height_devices * columns
    scale = 1.0 / math.sqrt(pixel_total)
    return (
        outputs[None],
        grad_inputs[None],
        spatial_sum * scale,
        temporal_sum * scale,
        gain_sum * scale,
        shift_sum * scale,
    )


def solution(mesh):
    in_specs = (
        P("rep", "tm", "height", None, None),
        P(),
        P(),
        P(),
        P(),
        P("rep", "tm", "height", None, None),
    )
    out_specs = (
        P("rep", "tm", "height", None, None),
        P("rep", "tm", "height", None, None),
        P(),
        P(),
        P(),
        P(),
    )
    return jax.shard_map(shards, mesh=mesh, in_specs=in_specs, out_specs=out_specs, check_vma=False)
```

profile of v0, /device:TPU:2, one launch (start us, length us, event | category | flops | bytes accessed | tf_op | source)
XLA Modules:
  0.0 734.6 jit_solution(1848081160454730432)
XLA Ops:
  7.2 0.8 fusion.138
  8.0 1.7 collective-permute-start
  9.8 1.3 collective-permute-start.1
  12.2 1.3 dynamic-slice
  14.2 1.4 select_maximum_fusion.2
  15.9 0.7 copy-done
  19.0 3.8 collective-permute-start.2
  23.1 4.7 collective-permute-done.2
  28.1 0.9 multiply_reduce_fusion
  29.1 0.8 reduce_sum.101
  29.9 1.4 reduce_sum.123
  32.0 0.9 reduce_sum.124
  32.9 15.0 %all-reduce.11 = (f32[4,32]{1,0:T(4,128)S(1)}, f32[4,32]{1,0:T(4,128)S(1)}) all-reduce(f32[4,32]{1,0:T(4,128)} %reduce_sum.120, f32[4,32]{1,0:T(4,128)S(1)} %reduce_sum.124), channel_id=1, replica_groups=mesh['rep'=4,'tm'=16,'height'=8] {'height'}, use_global_device_ids=true, to_apply=%region_2.3 | all-reduce | flops 256 | bytes 2048 | tf_op jit(solution)/shard_map/psum | solution.py:92
  48.4 37.0 %all-reduce.9 = (f32[512]{0:T(512)S(1)}, f32[512]{0:T(512)S(1)}) all-reduce(f32[512]{0:T(512)S(1)} %dynamic-update-slice, f32[512]{0:T(512)S(1)} %dynamic-update-slice.1), channel_id=2, replica_groups=mesh['rep'=4,'tm'=16,'height'=8] {'tm'}, use_global_device_ids=true, to_apply=%add.2 | all-reduce | flops 1024 | bytes 8192
  85.7 1.3 add_rsqrt_fusion
  88.3 0.8 sub.44
  89.1 0.7 sub.45
  89.9 1.5 fusion.30
  91.8 12.4 %all-reduce.10 = (f32[4,32]{1,0:T(4,128)S(1)}, f32[4,32]{1,0:T(4,128)S(1)}) all-reduce(f32[4,32]{1,0:T(4,128)S(1)} %reduce_sum.131, f32[4,32]{1,0:T(4,128)S(1)} %reduce_sum.128), channel_id=1, replica_groups=mesh['rep'=4,'tm'=16,'height'=8] {'height'}, use_global_device_ids=true, to_apply=%region_17.18 | all-reduce | flops 256 | bytes 2048 | tf_op jit(solution)/shard_map/psum | solution.py:117
  104.8 28.7 %all-reduce.8 = (f32[512]{0:T(512)S(1)}, f32[512]{0:T(512)S(1)}) all-reduce(f32[512]{0:T(512)S(1)} %dynamic-update-slice.2, f32[512]{0:T(512)S(1)} %dynamic-update-slice.3), channel_id=4, replica_groups=mesh['rep'=4,'tm'=16,'height'=8] {'tm'}, use_global_device_ids=true, to_apply=%add.4 | all-reduce | flops 1024 | bytes 8192
  134.9 2.7 fusion.28
  137.9 1.3 collective-permute-start.3
  139.2 99.2 %all-reduce.6 = (f32[128]{0:T(128)S(1)}, f32[128]{0:T(128)S(1)}) all-reduce(f32[128]{0:T(128)S(1)} %get-tuple-element.125, f32[128]{0:T(128)S(1)} %get-tuple-element.128), channel_id=1, replica_groups=mesh['rep'=4,'tm'=16,'height'=8] {'rep','tm','height'}, use_global_device_ids=true, to_apply=%region_27.28 | all-reduce | flops 256 | bytes 2048 | tf_op jit(solution)/shard_map/psum | solution.py:173
  240.6 1.2 fusion.50
  241.8 1.2 fusion.13
  246.4 1.7 collective-permute-start.4
  248.2 1.3 collective-permute-start.5
  250.2 0.8 copy-done.7
  251.0 1.2 collective-permute-done.5
  255.0 1.1 fusion.14
  256.1 469.0 %all-reduce.14.cloned.1.call-done = (f32[3,3,128,128]{3,2,1,0:T(8,128)}, f32[3,128,128]{2,1,0:T(8,128)}) async-done(((f32[3,3,128,128]{3,2,1,0:T(8,128)}, f32[3,128,128]{2,1,0:T(8,128)}), (f32[3,3,128,128]{3,2,1,0:T(8,128)}, f32[3,128,128]{2,1,0:T(8,128)})) %all-reduce.14.cloned.1.call-update) | async-done | bytes 786448 | tf_op jit(solution)/shard_map/psum | solution.py:173
  725.1 2.0 broadcast_multiply_fusion
  (143 shorter events, 19.8 us)
Async XLA Ops:
  7.2 8.4 %copy-start.3 = (bf16[3,3,128,128]{3,2,1,0:T(8,128)(2,1)S(1)}, bf16[3,3,128,128]{3,2,1,0:T(8,128)(2,1)}, u32[]{:S(2)}) copy-start(bf16[3,3,128,128]{3,2,1,0:T(8,128)(2,1)} %param.11) | copy-start | bytes 884740
  7.2 717.9 %all-reduce.14.cloned.1.call-start = ((), (), s32[]{:S(2)}) async-start(), calls=%async_computation | async-start | bytes 1572864 | tf_op jit(solution)/shard_map/psum | solution.py:173
  8.0 6.0 collective-permute-start
  9.8 4.5 collective-permute-start.1
  14.1 1.9 copy-start.10
  15.6 1.0 copy-start
  18.7 4.2 copy-start.8
  19.0 8.8 %collective-permute-start.2 = (bf16[2,16,32,128]{3,2,1,0:T(8,128)(2,1)S(1)}, bf16[2,16,32,128]{3,2,1,0:T(8,128)(2,1)S(1)}, u32[]{:S(2)}, u32[]{:S(2)}) collective-permute-start(bf16[2,16,32,128]{3,2,1,0:T(8,128)(2,1)S(1)} %slice.195), channel_id=1, source_target_pairs={{0,8},{8,16},{16,24},{24,32},{32,40},{40,48},{48,56},{56,64},{64,7... | collective-permute-start | bytes 786440 | tf_op jit(solution)/shard_map/ppermute | solution.py:27
  27.8 1.2 copy-start.5
  29.1 60.8 %copy-start.1 = (bf16[1,4,16,32,128]{4,3,2,1,0:T(8,128)(2,1)S(1)}, bf16[1,4,16,32,128]{4,3,2,1,0:T(8,128)(2,1)}, u32[]{:S(2)}) copy-start(bf16[1,4,16,32,128]{4,3,2,1,0:T(8,128)(2,1)} %param.15) | copy-start | bytes 1572868
  87.0 0.6 copy-start.12
  89.8 14.4 %copy-start.13 = (f32[4,32]{1,0:T(4,128)S(1)}, f32[4,32]{1,0:T(4,128)}, u32[]{:S(2)}) copy-start(f32[4,32]{1,0:T(4,128)} %copy-done.12) | copy-start | bytes 1540
  89.8 14.4 %copy-start.14 = (f32[4,32]{1,0:T(4,128)S(1)}, f32[4,32]{1,0:T(4,128)}, u32[]{:S(2)}) copy-start(f32[4,32]{1,0:T(4,128)} %get-tuple-element.172) | copy-start | bytes 1540
  89.8 14.4 %copy-start.19 = (f32[4]{0:T(128)S(1)}, f32[4]{0:T(128)}, u32[]{:S(2)}) copy-start(f32[4]{0:T(128)} %fusion.122) | copy-start | bytes 52
  89.8 14.4 %copy-start.20 = (f32[4]{0:T(128)S(1)}, f32[4]{0:T(128)}, u32[]{:S(2)}) copy-start(f32[4]{0:T(128)} %fusion.121) | copy-start | bytes 52
  89.8 45.0 %copy-start.15 = (f32[4,128]{1,0:T(4,128)S(1)}, f32[4,128]{1,0:T(4,128)}, u32[]{:S(2)}) copy-start(f32[4,128]{1,0:T(4,128)} %mul.190) | copy-start | bytes 6148
  89.8 45.0 %copy-start.16 = (f32[4,128]{1,0:T(4,128)S(1)}, f32[4,128]{1,0:T(4,128)}, u32[]{:S(2)}) copy-start(f32[4,128]{1,0:T(4,128)} %sub.45) | copy-start | bytes 6148
  89.9 45.0 %copy-start.17 = (f32[128]{0:T(128)S(1)}, f32[128]{0:T(128)}, u32[]{:S(2)}) copy-start(f32[128]{0:T(128)} %param.13) | copy-start | bytes 1540
  89.9 45.0 %copy-start.18 = (f32[128]{0:T(128)S(1)}, f32[128]{0:T(128)}, u32[]{:S(2)}) copy-start(f32[128]{0:T(128)} %param.14) | copy-start | bytes 1540
  137.6 101.4 %copy-start.6 = (bf16[2,16,32,128]{3,2,1,0:T(8,128)(2,1)S(1)}, bf16[2,16,32,128]{3,2,1,0:T(8,128)(2,1)}, u32[]{:S(2)}) copy-start(bf16[2,16,32,128]{3,2,1,0:T(8,128)(2,1)} %copy-done.5) | copy-start | bytes 786436
  137.9 102.7 %collective-permute-start.3 = (bf16[2,16,32,128]{3,2,1,0:T(8,128)(2,1)S(1)}, bf16[2,16,32,128]{3,2,1,0:T(8,128)(2,1)}, u32[]{:S(2)}, u32[]{:S(2)}) collective-permute-start(bf16[2,16,32,128]{3,2,1,0:T(8,128)(2,1)S(1)} %slice.196), channel_id=1, source_target_pairs={{8,0},{16,8},{24,16},{32,24},{40,32},{48,40},{56,48},{64,56},{72,6... | collective-permute-start | bytes 786440 | tf_op jit(solution)/shard_map/ppermute | solution.py:27
  243.1 1.0 copy-start.4
  243.5 0.9 copy-start.11
  246.4 4.6 collective-permute-start.4
  248.2 4.0 collective-permute-start.5
  250.2 0.8 copy-start.7
  251.0 1.6 copy-start.2
  725.1 2.0 copy-start.9
Sparse Core Ops, SparseCore 0:
  251.1 473.9 all-reduce.13
where the time goes:
time: 735 us
  waiting for transfers between devices  475 us (65%)
  blocking collectives  192 us (26%)
  between operations  15.2 us (2%)
  matrix products  14.7 us (2%)
  other arithmetic  14.4 us (2%)
  local copies, waits for them, and re-layouts  11.3 us (2%)
  starting transfers between devices  11.2 us (2%)
    psum x1, waiting for transfers between devices, shards(): lax.psum((spatial_part, temporal_part, gain_part, shift_part), ('rep', 't...  469 us
    psum x1, blocking collectives, shards(): lax.psum((spatial_part, temporal_part, gain_part, shift_part), ('rep', 't...  99.2 us
    unnamed x2, blocking collectives  65.7 us
    psum x1, blocking collectives, shards(): row_first, row_second = lax.psum((first, second), 'height')  15 us
  transfers between devices with their start and end apart: 7, of which 4 were waited for; matrix products, arithmetic and copies ran while one was open for 1% of the time, Pallas kernels for 0%

commit v1 on v0

--- a/solution.py
+++ b/solution.py
@@ -171,7 +171,7 @@
     spatial_part = jnp.stack(spatial_terms).reshape(3, 3, channels, channels)
     grad_inputs = grad_in.astype(jnp.bfloat16)
     spatial_sum, temporal_sum, gain_sum, shift_sum = lax.psum(
-        (spatial_part, temporal_part, gain_part, shift_part), ("rep", "tm", "height")
+        lax.psum((spatial_part, temporal_part, gain_part, shift_part), "rep"), ("tm", "height")
     )
     pixel_total = lax.axis_size("rep") * frames * time_devices * rows * height_devices * columns
     scale = 1.0 / math.sqrt(pixel_total)

time: 735 us -> 817 us (1.11)
  blocking collectives: 192 us -> 348 us
  waiting for transfers between devices: 475 us -> 399 us
    psum x1 -> x2, blocking collectives: 99.2 us -> 255 us  [the longest x1 247 us: shards(): lax.psum(lax.psum((spatial_part, temporal_part, gain_part, shift_part), '...]
    psum x1 -> x2, waiting for transfers between devices: 469 us -> 393 us  [the longest x1 342 us: shards(): lax.psum(lax.psum((spatial_part, temporal_part, gain_part, shift_part), '...]
  transfers between devices with their start and end apart: 7 -> 8, of which waited for: 4 -> 5; matrix products, arithmetic and copies ran while one was open for 1% -> 1% of each run, Pallas kernels for 0% -> 0%
where the time goes in v1:
time: 817 us; the launch traced here: 816 us
  waiting for transfers between devices  399 us (49%)
  blocking collectives  348 us (43%)
  between operations  15.2 us (2%)
  other arithmetic  14.9 us (2%)
  matrix products  13.7 us (2%)
  local copies, waits for them, and re-layouts  13 us (2%)
  starting transfers between devices  11.5 us (1%)
    psum x1, waiting for transfers between devices, shards(): lax.psum(lax.psum((spatial_part, temporal_part, gain_part, shift_part), '...  342 us
    psum x1, blocking collectives, shards(): lax.psum(lax.psum((spatial_part, temporal_part, gain_part, shift_part), '...  247 us
    unnamed x2, blocking collectives  65.7 us
    psum x1, waiting for transfers between devices, shards(): lax.psum((spatial_part, temporal_part, gain_part, shift_part), 'rep')  51 us
  transfers between devices with their start and end apart: 8, of which 5 were waited for; matrix products, arithmetic and copies ran while one was open for 1% of the time, Pallas kernels for 0%

profile of v1, /device:TPU:2, one launch (start us, length us, event | category | flops | bytes accessed | tf_op | source)
XLA Modules:
  0.0 815.8 jit_solution(8473787645335572052)
XLA Ops:
  7.2 0.8 fusion.138
  8.0 1.7 collective-permute-start
  9.8 1.3 collective-permute-start.1
  12.2 1.3 dynamic-slice
  14.2 1.4 select_maximum_fusion.2
  19.0 3.8 collective-permute-start.2
  23.1 4.7 collective-permute-done.2
  28.1 0.9 multiply_reduce_fusion
  29.1 0.8 reduce_sum.101
  29.9 1.4 reduce_sum.123
  32.0 0.9 reduce_sum.124
  32.9 15.0 %all-reduce.11 = (f32[4,32]{1,0:T(4,128)S(1)}, f32[4,32]{1,0:T(4,128)S(1)}) all-reduce(f32[4,32]{1,0:T(4,128)} %reduce_sum.120, f32[4,32]{1,0:T(4,128)S(1)} %reduce_sum.124), channel_id=1, replica_groups=mesh['rep'=4,'tm'=16,'height'=8] {'height'}, use_global_device_ids=true, to_apply=%region_2.3 | all-reduce | flops 256 | bytes 2048 | tf_op jit(solution)/shard_map/psum | solution.py:92
  48.4 37.0 %all-reduce.9 = (f32[512]{0:T(512)S(1)}, f32[512]{0:T(512)S(1)}) all-reduce(f32[512]{0:T(512)S(1)} %dynamic-update-slice, f32[512]{0:T(512)S(1)} %dynamic-update-slice.1), channel_id=2, replica_groups=mesh['rep'=4,'tm'=16,'height'=8] {'tm'}, use_global_device_ids=true, to_apply=%add.2 | all-reduce | flops 1024 | bytes 8192
  85.7 1.3 add_rsqrt_fusion
  88.3 0.8 sub.44
  89.9 2.0 fusion.30
  92.3 12.4 %all-reduce.10 = (f32[4,32]{1,0:T(4,128)S(1)}, f32[4,32]{1,0:T(4,128)S(1)}) all-reduce(f32[4,32]{1,0:T(4,128)S(1)} %reduce_sum.131, f32[4,32]{1,0:T(4,128)S(1)} %reduce_sum.128), channel_id=1, replica_groups=mesh['rep'=4,'tm'=16,'height'=8] {'height'}, use_global_device_ids=true, to_apply=%region_17.18 | all-reduce | flops 256 | bytes 2048 | tf_op jit(solution)/shard_map/psum | solution.py:117
  105.3 28.7 %all-reduce.8 = (f32[512]{0:T(512)S(1)}, f32[512]{0:T(512)S(1)}) all-reduce(f32[512]{0:T(512)S(1)} %dynamic-update-slice.2, f32[512]{0:T(512)S(1)} %dynamic-update-slice.3), channel_id=4, replica_groups=mesh['rep'=4,'tm'=16,'height'=8] {'tm'}, use_global_device_ids=true, to_apply=%add.4 | all-reduce | flops 1024 | bytes 8192
  135.4 2.7 fusion.28
  138.5 1.3 collective-permute-start.3
  139.8 8.6 %all-reduce.12 = (f32[128]{0:T(128)S(1)}, f32[128]{0:T(128)S(1)}) all-reduce(f32[128]{0:T(128)S(1)} %copy-done.21, f32[128]{0:T(128)S(1)} %copy-done.22), channel_id=1, replica_groups=mesh['rep'=4,'tm'=16,'height'=8] {'rep'}, use_global_device_ids=true, to_apply=%region_29.30 | all-reduce | flops 256 | bytes 2048 | tf_op jit(solution)/shard_map/psum | solution.py:174
  148.4 246.8 %all-reduce.6 = (f32[128]{0:T(128)S(1)}, f32[128]{0:T(128)S(1)}) all-reduce(f32[128]{0:T(128)S(1)} %get-tuple-element.167, f32[128]{0:T(128)S(1)} %get-tuple-element.168), channel_id=1, replica_groups=mesh['rep'=4,'tm'=16,'height'=8] {'tm','height'}, use_global_device_ids=true, to_apply=%region_30.31 | all-reduce | flops 256 | bytes 2048 | tf_op jit(solution)/shard_map/psum | solution.py:173
  398.9 1.3 fusion.73
  402.3 1.8 collective-permute-start.4
  404.1 1.5 collective-permute-start.5
  406.3 0.8 copy-done.8
  409.0 0.7 copy-done.2
  410.0 0.9 copy-done.3
  411.4 51.0 %all-reduce.19.cloned.1.call-done = (f32[3,3,128,128]{3,2,1,0:T(8,128)}, f32[3,128,128]{2,1,0:T(8,128)}) async-done(((f32[3,3,128,128]{3,2,1,0:T(8,128)}, f32[3,128,128]{2,1,0:T(8,128)}), (f32[3,3,128,128]{3,2,1,0:T(8,128)}, f32[3,128,128]{2,1,0:T(8,128)})) %all-reduce.19.cloned.1.call-update) | async-done | bytes 786448 | tf_op jit(solution)/shard_map/psum | solution.py:174
  462.7 1.1 fusion.14
  463.8 342.5 %all-reduce.17.cloned.1.call-done = (f32[3,3,128,128]{3,2,1,0:T(8,128)}, f32[3,128,128]{2,1,0:T(8,128)}) async-done(((f32[3,3,128,128]{3,2,1,0:T(8,128)}, f32[3,128,128]{2,1,0:T(8,128)}), (f32[3,3,128,128]{3,2,1,0:T(8,128)}, f32[3,128,128]{2,1,0:T(8,128)})) %all-reduce.17.cloned.1.call-update) | async-done | bytes 786448 | tf_op jit(solution)/shard_map/psum | solution.py:173
  806.3 2.0 broadcast_multiply_fusion
  (153 shorter events, 21.7 us)
Async XLA Ops:
  7.2 8.4 %copy-start.4 = (bf16[3,3,128,128]{3,2,1,0:T(8,128)(2,1)S(1)}, bf16[3,3,128,128]{3,2,1,0:T(8,128)(2,1)}, u32[]{:S(2)}) copy-start(bf16[3,3,128,128]{3,2,1,0:T(8,128)(2,1)} %param.11) | copy-start | bytes 884740
  7.2 455.2 %all-reduce.19.cloned.1.call-start = ((), (), s32[]{:S(2)}) async-start(), calls=%async_computation.1 | async-start | bytes 1572864 | tf_op jit(solution)/shard_map/psum | solution.py:174
  8.0 6.0 collective-permute-start
  9.8 4.5 collective-permute-start.1
  14.1 1.9 copy-start.11
  15.6 1.0 copy-start
  18.7 4.2 copy-start.9
  19.0 8.8 %collective-permute-start.2 = (bf16[2,16,32,128]{3,2,1,0:T(8,128)(2,1)S(1)}, bf16[2,16,32,128]{3,2,1,0:T(8,128)(2,1)S(1)}, u32[]{:S(2)}, u32[]{:S(2)}) collective-permute-start(bf16[2,16,32,128]{3,2,1,0:T(8,128)(2,1)S(1)} %slice.195), channel_id=1, source_target_pairs={{0,8},{8,16},{16,24},{24,32},{32,40},{40,48},{48,56},{56,64},{64,7... | collective-permute-start | bytes 786440 | tf_op jit(solution)/shard_map/ppermute | solution.py:27
  27.8 1.2 copy-start.6
  29.1 60.8 %copy-start.1 = (bf16[1,4,16,32,128]{4,3,2,1,0:T(8,128)(2,1)S(1)}, bf16[1,4,16,32,128]{4,3,2,1,0:T(8,128)(2,1)}, u32[]{:S(2)}) copy-start(bf16[1,4,16,32,128]{4,3,2,1,0:T(8,128)(2,1)} %param.15) | copy-start | bytes 1572868
  87.0 0.6 copy-start.13
  89.8 14.9 %copy-start.14 = (f32[4,32]{1,0:T(4,128)S(1)}, f32[4,32]{1,0:T(4,128)}, u32[]{:S(2)}) copy-start(f32[4,32]{1,0:T(4,128)} %copy-done.13) | copy-start | bytes 1540
  89.8 14.9 %copy-start.15 = (f32[4,32]{1,0:T(4,128)S(1)}, f32[4,32]{1,0:T(4,128)}, u32[]{:S(2)}) copy-start(f32[4,32]{1,0:T(4,128)} %get-tuple-element.176) | copy-start | bytes 1540
  89.8 14.9 %copy-start.20 = (f32[4]{0:T(128)S(1)}, f32[4]{0:T(128)}, u32[]{:S(2)}) copy-start(f32[4]{0:T(128)} %fusion.122) | copy-start | bytes 52
  89.8 14.9 %copy-start.23 = (f32[4]{0:T(128)S(1)}, f32[4]{0:T(128)}, u32[]{:S(2)}) copy-start(f32[4]{0:T(128)} %fusion.121) | copy-start | bytes 52
  89.8 45.5 %copy-start.16 = (f32[4,128]{1,0:T(4,128)S(1)}, f32[4,128]{1,0:T(4,128)}, u32[]{:S(2)}) copy-start(f32[4,128]{1,0:T(4,128)} %mul.190) | copy-start | bytes 6148
  89.8 45.5 %copy-start.17 = (f32[4,128]{1,0:T(4,128)S(1)}, f32[4,128]{1,0:T(4,128)}, u32[]{:S(2)}) copy-start(f32[4,128]{1,0:T(4,128)} %sub.45) | copy-start | bytes 6148
  89.9 45.5 %copy-start.18 = (f32[128]{0:T(128)S(1)}, f32[128]{0:T(128)}, u32[]{:S(2)}) copy-start(f32[128]{0:T(128)} %param.13) | copy-start | bytes 1540
  89.9 45.5 %copy-start.19 = (f32[128]{0:T(128)S(1)}, f32[128]{0:T(128)}, u32[]{:S(2)}) copy-start(f32[128]{0:T(128)} %param.14) | copy-start | bytes 1540
  138.1 1.7 copy-start.21
  138.1 1.7 copy-start.22
  138.1 257.6 %copy-start.7 = (bf16[2,16,32,128]{3,2,1,0:T(8,128)(2,1)S(1)}, bf16[2,16,32,128]{3,2,1,0:T(8,128)(2,1)}, u32[]{:S(2)}) copy-start(bf16[2,16,32,128]{3,2,1,0:T(8,128)(2,1)} %copy-done.6) | copy-start | bytes 786436
  138.5 258.9 %collective-permute-start.3 = (bf16[2,16,32,128]{3,2,1,0:T(8,128)(2,1)S(1)}, bf16[2,16,32,128]{3,2,1,0:T(8,128)(2,1)S(1)}, u32[]{:S(2)}, u32[]{:S(2)}) collective-permute-start(bf16[2,16,32,128]{3,2,1,0:T(8,128)(2,1)S(1)} %slice.196), channel_id=1, source_target_pairs={{8,0},{16,8},{24,16},{32,24},{40,32},{48,40},{56,48},{64,56},{72,6... | collective-permute-start | bytes 786440 | tf_op jit(solution)/shard_map/ppermute | solution.py:27
  398.0 1.0 copy-start.5
  398.3 1.9 copy-start.12
  402.3 4.9 collective-permute-start.4
  404.1 3.3 collective-permute-start.5
  406.3 0.8 copy-start.8
  407.1 399.2 %all-reduce.17.cloned.1.call-start = ((), (), s32[]{:S(2)}) async-start(), calls=%async_computation | async-start | bytes 1572864 | tf_op jit(solution)/shard_map/psum | solution.py:173
  408.6 1.0 copy-start.2
  409.7 1.2 copy-start.3
  806.3 2.0 copy-start.10
Sparse Core Ops, SparseCore 0:
  407.2 55.1 all-reduce.18
  465.9 340.3 all-reduce.16
